TPU v7x, 32 devices: a whole 2x2x4 slice. The times are simulated.
32 devices in a mesh: doc: 4 (over z), feat: 8 (over y, x, core).
Axes of the slice: x: 2, y: 2, z: 4, core: 2. Of those that a mesh axis runs over, the one named last changes fastest.
Arguments:
- documents: bfloat16 [512, 512], P('doc', 'feat'), may hold values from -6 to 6
- directions: bfloat16 [512, 32768], P('doc', 'feat'), may hold values from -0.5 to 0.5
- phase: float32 [32768], P('feat'), may hold values from -3.140625 to 3.140625
- amplitude: float32 [32768], P('feat'), may hold values from 0.4 to 2.3
- doc_weight: float32 [512], P('doc'), may hold values from 0.5 to 4.2
- labels: int32 [512], P('doc'), may hold values from 0 to 127
Outputs:
- margins: float32 [512, 128], P('doc')
- scaled_weights: float32 [32768, 128], P('feat')
All inputs are finite; a program needn't handle non-finite values.
Results may differ from a plain program's by a relative error of at most 0.0003.
Values may be sent and summed in bfloat16 or wider, within the bound.
A program may use at most 64 MiB of HBM per device.

v0:
```python
import jax
import jax.numpy as jnp
from jax import lax
from jax.sharding import PartitionSpec as P

C = 128
ITERS = 3
NEWTON = 3
HI = lax.Precision.HIGHEST
shrink_level = 0.1
ratio_floor = 1e-06


def logistic_prox(target, signs, weight_ratio):
    current = target
    for newton_step in range(NEWTON):
        chance = jax.nn.sigmoid(-signs * current)
        gradient = current - target - weight_ratio * signs * chance
        current = current - gradient / (1.0 + weight_ratio * chance * (1.0 - chance))
    return current


def shrink_values(target, limit):
    return target - jnp.clip(target, -limit, limit)


def per_device(documents, directions, phase, amplitude, doc_weight, labels):
    doc_count = documents.shape[0]
    width_tile = directions.shape[1]
    num_feat = lax.axis_size("feat")
    num_doc = lax.axis_size("doc")
    chunk = width_tile // num_doc
    row = lax.axis_index("doc")
    doc_rows = lax.all_gather(documents, "feat", axis=1, tiled=True)
    doc_full = lax.all_gather(doc_rows, "doc", axis=0, tiled=True)
    dir_chunk = lax.all_to_all(directions, "doc", split_axis=1, concat_axis=0, tiled=True)
    phase_c = lax.dynamic_slice_in_dim(phase, row * chunk, chunk, 0)
    amp_c = lax.dynamic_slice_in_dim(amplitude, row * chunk, chunk, 0)
    angles = jnp.dot(doc_full, dir_chunk, preferred_element_type=jnp.float32)
    features = jnp.sqrt(2.0 / width_tile) * amp_c * jnp.cos(angles + phase_c)
    blocks = features.reshape(num_doc, doc_count, chunk)
    gram = jnp.einsum("iac,ibc->iab", blocks, blocks, precision=HI)
    gram = lax.psum_scatter(gram, "doc", scatter_dimension=0, tiled=True)[0]
    eye = jnp.eye(doc_count, dtype=jnp.float32)
    factor = jnp.linalg.cholesky(eye + gram)
    lower_inv = lax.linalg.triangular_solve(factor, eye, left_side=True, lower=True)
    inverse = lax.dot_general(lower_inv, lower_inv, (((0,), (0,)), ((), ())), precision=HI)
    signs = jnp.where(labels[:, None] == jnp.arange(C, dtype=jnp.int32)[None, :], 1.0, -1.0).astype(
        jnp.float32
    )
    share_rows = doc_count // num_feat
    offset = lax.axis_index("feat") * share_rows
    signs = lax.dynamic_slice_in_dim(signs, offset, share_rows, 0)
    weight = lax.dynamic_slice_in_dim(doc_weight, offset, share_rows, 0)[:, None]
    rho = jnp.float32(1.0)
    margins = logistic_prox(jnp.zeros(signs.shape, jnp.float32), signs, weight / rho)
    sums = jnp.zeros(signs.shape, jnp.float32)
    duals_y = jnp.zeros(signs.shape, jnp.float32)
    part = jnp.zeros((doc_count, C), jnp.float32)
    image = jnp.zeros((doc_count, C), jnp.float32)
    weights = jnp.zeros((chunk, C), jnp.float32)
    product = jnp.zeros((doc_count, C), jnp.float32)
    for step in range(ITERS):
        correction = (margins - duals_y - sums) / num_feat
        correction = lax.all_gather(correction, "feat", axis=0, tiled=True)
        target = part + correction
        residue = target - image
        solved = jnp.dot(inverse, residue, precision=HI)
        applied = residue - solved
        part = target - solved
        sums = lax.psum_scatter(part, "feat", scatter_dimension=0, tiled=True)
        all_solved = lax.all_gather(solved, "doc", axis=0, tiled=True)
        lifted = lax.dot_general(features, all_solved, (((0,), (0,)), ((), ())), precision=HI)
        old_weights = weights
        old_margins = margins
        weights = shrink_values(weights + lifted / num_doc, shrink_level / (rho * num_doc))
        margins = logistic_prox(sums + duals_y, signs, weight / rho)
        duals_y = duals_y + sums - margins
        if step + 1 < ITERS:
            move = old_weights - weights
            if step == 0:
                d_move, d_solved, d_applied, d_lifted = (move, solved, applied, lifted)
            else:
                d_move = move - last_move / growth
                d_solved = solved - last_solved / growth
                d_applied = applied - last_applied / growth
                d_lifted = lifted - last_lifted / growth
            primal = (
                jnp.sum(num_doc * d_move * d_move + 2.0 * d_move * d_lifted)
                + jnp.sum(d_solved * d_applied)
                + jnp.sum((sums - margins) ** 2)
            )
            dual = num_doc * jnp.sum(move**2) + jnp.sum((margins - old_margins) ** 2)
            primal, dual = lax.psum((primal, dual), ("doc", "feat"))
            primal = jnp.maximum(primal, 0.0)
            new_product = jnp.dot(features, weights, precision=HI)
            new_product = lax.psum_scatter(new_product, "doc", scatter_dimension=0, tiled=True)
            growth = ((primal + ratio_floor) / (rho * rho * dual + ratio_floor)) ** 0.25
            rho = rho * growth
            duals_y = duals_y / growth
            image = new_product - (product - new_product + applied) / growth
            product = new_product
            last_move, last_solved, last_applied, last_lifted = (move, solved, applied, lifted)
    margins = lax.all_gather(margins, "feat", axis=0, tiled=True)
    weights = lax.all_gather(num_feat * weights, "doc", axis=0, tiled=True)
    return (margins, weights)


def solution(mesh):
    in_specs = (P("doc", "feat"), P("doc", "feat"), P("feat"), P("feat"), P("doc"), P("doc"))
    out_specs = (P("doc", None), P("feat", None))
    return jax.shard_map(
        per_device, mesh=mesh, in_specs=in_specs, out_specs=out_specs, check_vma=False
    )
```

profile of v0, /device:TPU:0, one launch (start us, length us, event | category | flops | bytes accessed | tf_op | source)
XLA Modules:
  0.0 383.9 jit_solution(2985545460666034803)
XLA Ops:
  7.2 2.3 copy.10
  9.4 6.3 %all-to-all-start = ((bf16[128,4,1024]{0,2,1:T(8,128)(2,1)}), bf16[128,4,1024]{0,2,1:T(8,128)(2,1)S(1)}, u32[]{:S(2)}, u32[]{:S(2)}) async-start(bf16[128,4,1024]{0,2,1:T(8,128)(2,1)} %bitcast), calls=%async_computation | async-start | bytes 2097152 | tf_op jit(solution)/shard_map/all_to_all | solution.py:36
  15.8 9.2 %all_gather.31 = bf16[128,512]{0,1:T(8,128)(2,1)S(1)} all-gather(bf16[128,64]{0,1:T(8,128)(2,1)S(1)} %copy-done.4), channel_id=1, replica_groups=mesh['doc'=4,'feat'=8] {'feat'}, dimensions={1}, use_global_device_ids=true | all-gather | bytes 147456 | tf_op jit(solution)/shard_map/all_gather | solution.py:34
  25.7 25.3 %all_gather.32 = bf16[512,512]{0,1:T(8,128)(2,1)} all-gather(bf16[128,512]{0,1:T(8,128)(2,1)S(1)} %all_gather.31), channel_id=1, replica_groups=mesh['doc'=4,'feat'=8] {'doc'}, dimensions={0}, use_global_device_ids=true | all-gather | bytes 655360 | tf_op jit(solution)/shard_map/all_gather | solution.py:35
  51.6 8.3 %cosine_multiply_fusion = f32[512,1024]{1,0:T(8,128)S(1)} fusion(bf16[512,512]{0,1:T(8,128)(2,1)} %all_gather.32, bf16[512,1024]{1,0:T(8,128)(2,1)S(1)} %bitcast.38, f32[1024]{0:T(1024)S(1)} %dynamic-slice-done, f32[1024]{0:T(1024)S(1)} %dynamic-slice_multiply_fusion), kind=kOutput, calls=%fused_computation | convolution fusion | flops 537919488 | bytes 3678208 | tf_op jit(solution)/shard_map/dot_general | solution.py:39
  59.9 2.8 fusion.142
  63.1 9.4 %all_gather.30 = f32[128,128]{1,0:T(8,128)S(1)} all-gather(f32[16,128]{1,0:T(8,128)S(1)} %broadcast_multiply_fusion), channel_id=1, replica_groups=mesh['doc'=4,'feat'=8] {'feat'}, dimensions={0}, use_global_device_ids=true | all-gather | bytes 73728 | tf_op jit(solution)/shard_map/all_gather | solution.py:65
  72.5 14.2 %reduce-scatter.7.cloned.1.call-done = f32[1,128,128]{2,1,0:T(8,128)} async-done(((f32[4,128,128]{2,1,0:T(8,128)}), f32[1,128,128]{2,1,0:T(8,128)}) %reduce-scatter.7.cloned.1.call-update) | async-done | bytes 65552 | tf_op jit(solution)/shard_map/reduce_scatter | solution.py:43
  88.5 11.7 %cholesky.18 = f32[128,128]{1,0:T(8,128)S(1)} custom-call(f32[128,128]{1,0:T(8,128)S(1)} %fusion.13), custom_call_target="Cholesky" | custom-call | tf_op jit(solution)/shard_map/jit(cholesky)/cholesky | solution.py:45
  101.6 9.8 %custom-call.6 = f32[1,128,128]{1,2,0:T(8,128)S(1)} custom-call(f32[1,128,128]{2,1,0:T(8,128)S(1)} %fusion.10), custom_call_target="InvertDiagBlocksLowerTriangular" | custom-call | tf_op jit(solution)/shard_map/triangular_solve | solution.py:46
  111.9 1.5 multiply_reduce_fusion.3
  113.5 14.1 %all_gather.33 = f32[512,128]{1,0:T(8,128)S(1)} all-gather(f32[128,128]{1,0:T(8,128)S(1)} %get-tuple-element.23), channel_id=1, replica_groups=mesh['doc'=4,'feat'=8] {'doc'}, dimensions={0}, use_global_device_ids=true | all-gather | bytes 327680 | tf_op jit(solution)/shard_map/all_gather | solution.py:72
  127.6 4.1 %multiply_reduce_fusion.1 = (f32[]{:T(128)}, f32[]{:T(128)}, f32[1024,128]{1,0:T(8,128)S(1)}) fusion(f32[512,1024]{1,0:T(8,128)S(1)} %cosine_multiply_fusion, f32[512,128]{1,0:T(8,128)S(1)} %all_gather.33), kind=kOutput, calls=%fused_computation.13 | convolution fusion | flops 806879232 | bytes 2883592 | tf_op jit(solution)/shard_map/dot_general | solution.py:73
  131.7 2.5 fusion.6
  136.2 9.2 %reduce-scatter.9.cloned.1.call-done = f32[16,128]{1,0:T(8,128)} async-done(((f32[128,128]{1,0:T(8,128)}), f32[16,128]{1,0:T(8,128)}) %reduce-scatter.9.cloned.1.call-update) | async-done | bytes 8208 | tf_op jit(solution)/shard_map/reduce_scatter | solution.py:71
  149.3 39.3 %all-reduce.1 = (f32[]{:T(128)}, f32[]{:T(128)}) all-reduce(f32[]{:T(128)S(6)} %add.203, f32[]{:T(128)S(6)} %add.205), channel_id=1, replica_groups=mesh['doc'=4,'feat'=8] {'doc','feat'}, use_global_device_ids=true, to_apply=%region_7.8 | all-reduce | flops 2 | bytes 16 | tf_op jit(solution)/shard_map/psum | solution.py:94
  190.6 10.2 %all_gather.34 = f32[128,128]{1,0:T(8,128)S(1)} all-gather(f32[16,128]{1,0:T(8,128)S(1)} %subtract_multiply_fusion.2), channel_id=1, replica_groups=mesh['doc'=4,'feat'=8] {'feat'}, dimensions={0}, use_global_device_ids=true | all-gather | bytes 73728 | tf_op jit(solution)/shard_map/all_gather | solution.py:65
  201.7 1.5 multiply_reduce_fusion.2
  203.2 14.2 %all_gather.35 = f32[512,128]{1,0:T(8,128)S(1)} all-gather(f32[128,128]{1,0:T(8,128)S(1)} %get-tuple-element.25), channel_id=1, replica_groups=mesh['doc'=4,'feat'=8] {'doc'}, dimensions={0}, use_global_device_ids=true | all-gather | bytes 327680 | tf_op jit(solution)/shard_map/all_gather | solution.py:72
  217.4 4.2 %multiply_reduce_fusion = (f32[]{:T(128)}, f32[]{:T(128)}, f32[1024,128]{1,0:T(8,128)S(1)}) fusion(f32[1024,128]{1,0:T(8,128)S(1)} %get-tuple-element.24, f32[]{:T(128)S(6)} %neg.66, f32[]{:T(128)S(6)} %div.199, f32[]{:T(128)S(6)} %pow.6, f32[512,1024]{1,0:T(8,128)S(1)} %cosine_multiply_fusion, f32[512,128]{1,0:T(8,128)S(1)} %all_gather.35), kind=kOutput, calls=%fused_computation.11 | convolution fusion | flops 808189952 | bytes 3407892 | tf_op jit(solution)/shard_map/dot_general | solution.py:73
  221.6 2.5 fusion.137
  226.1 9.7 %reduce-scatter.13.cloned.1.call-done = f32[16,128]{1,0:T(8,128)} async-done(((f32[128,128]{1,0:T(8,128)}), f32[16,128]{1,0:T(8,128)}) %reduce-scatter.13.cloned.1.call-update) | async-done | bytes 8208 | tf_op jit(solution)/shard_map/reduce_scatter | solution.py:71
  235.9 1.5 multiply_reduce_fusion.4
  238.5 39.4 %all-reduce = (f32[]{:T(128)}, f32[]{:T(128)}) all-reduce(f32[]{:T(128)S(6)} %add.219, f32[]{:T(128)S(6)} %add.221), channel_id=1, replica_groups=mesh['doc'=4,'feat'=8] {'doc','feat'}, use_global_device_ids=true, to_apply=%region_16.17 | all-reduce | flops 2 | bytes 16 | tf_op jit(solution)/shard_map/psum | solution.py:94
  279.9 11.2 %all_gather.36 = f32[128,128]{1,0:T(8,128)} all-gather(f32[16,128]{1,0:T(8,128)S(1)} %subtract_multiply_fusion.1), channel_id=1, replica_groups=mesh['doc'=4,'feat'=8] {'feat'}, dimensions={0}, use_global_device_ids=true | all-gather | bytes 73728 | tf_op jit(solution)/shard_map/all_gather | solution.py:65
  291.1 1.8 fusion.140
  292.9 14.0 %all_gather.38 = f32[512,128]{1,0:T(8,128)S(1)} all-gather(f32[128,128]{1,0:T(8,128)S(1)} %get-tuple-element.28), channel_id=1, replica_groups=mesh['doc'=4,'feat'=8] {'doc'}, dimensions={0}, use_global_device_ids=true | all-gather | bytes 327680 | tf_op jit(solution)/shard_map/all_gather | solution.py:72
  306.9 4.2 %subtract_multiply_fusion = f32[1024,128]{1,0:T(8,128)} fusion(f32[512,1024]{1,0:T(8,128)S(1)} %cosine_multiply_fusion, f32[512,128]{1,0:T(8,128)S(1)} %all_gather.38, f32[]{:T(128)S(6)} %neg.70, f32[]{:T(128)S(6)} %div.220, f32[]{:T(128)S(6)} %neg.66, f32[]{:T(128)S(6)} %div.199, f32[1024,128]{1,0:T(8,128)S(1)} %get-tuple-element.26, ...), kind=kOutput, calls=%fused_computation.10 | convolution fusion | flops 807141376 | bytes 3932176 | tf_op jit(solution)/shard_map/dot_general | solution.py:73
  311.2 14.3 %reduce-scatter.17.cloned.1.call-done = f32[16,128]{1,0:T(8,128)} async-done(((f32[128,128]{1,0:T(8,128)}), f32[16,128]{1,0:T(8,128)}) %reduce-scatter.17.cloned.1.call-update) | async-done | bytes 8208 | tf_op jit(solution)/shard_map/reduce_scatter | solution.py:71
  326.4 9.2 %all_gather.37 = f32[128,128]{1,0:T(8,128)S(1)} all-gather(f32[16,128]{1,0:T(8,128)S(1)} %fusion.63), channel_id=1, replica_groups=mesh['doc'=4,'feat'=8] {'feat'}, dimensions={0}, use_global_device_ids=true | all-gather | bytes 73728 | tf_op jit(solution)/shard_map/all_gather | solution.py:104
  335.6 37.8 %all-gather.2.cloned.1.call-done = f32[4096,128]{1,0:T(8,128)} async-done(((f32[1024,128]{1,0:T(8,128)}), f32[4096,128]{1,0:T(8,128)}) %all-gather.2.cloned.1.call-update) | async-done | bytes 2097168 | tf_op jit(solution)/shard_map/all_gather | solution.py:105
  374.0 3.0 copy.16
  (61 shorter events, 12.3 us)
Async XLA Ops:
  7.2 8.6 %copy-start.4 = (bf16[128,64]{0,1:T(8,128)(2,1)S(1)}, bf16[128,64]{0,1:T(8,128)(2,1)}, u32[]{:S(2)}) copy-start(bf16[128,64]{0,1:T(8,128)(2,1)} %param.6) | copy-start | bytes 49156
  9.4 41.6 %all-to-all-start = ((bf16[128,4,1024]{0,2,1:T(8,128)(2,1)}), bf16[128,4,1024]{0,2,1:T(8,128)(2,1)S(1)}, u32[]{:S(2)}, u32[]{:S(2)}) async-start(bf16[128,4,1024]{0,2,1:T(8,128)(2,1)} %bitcast), calls=%async_computation | async-start | bytes 2097152 | tf_op jit(solution)/shard_map/all_to_all | solution.py:36
  15.8 70.9 %reduce-scatter.7.cloned.1.call-start = ((), (), s32[]{:S(2)}) async-start(), calls=%async_computation.7 | async-start | bytes 327680 | tf_op jit(solution)/shard_map/reduce_scatter | solution.py:43
  15.8 35.8 %dynamic-slice-start = ((f32[4096]{0:T(1024)}, s32[]{:T(128)}), f32[1024]{0:T(1024)S(1)}, s32[]{:S(2)}) async-start(f32[4096]{0:T(1024)} %param.8, s32[]{:T(128)} %select_n.18), calls=%async_computation.14 | async-start | bytes 8704 | tf_op jit(solution)/shard_map/dynamic_slice | solution.py:37
  59.9 2.9 copy-start.9
  59.9 2.9 copy-start.7
  62.7 82.6 %reduce-scatter.9.cloned.1.call-start = ((), (), s32[]{:S(2)}) async-start(), calls=%async_computation.8 | async-start | bytes 73728 | tf_op jit(solution)/shard_map/reduce_scatter | solution.py:71
  62.9 173.0 %copy-start.5 = (s32[16]{0:T(128)}, s32[16]{0:T(128)S(1)}, u32[]{:S(2)}) copy-start(s32[16]{0:T(128)S(1)} %dynamic-slice) | copy-start | bytes 196
  113.5 87.4 %reduce-scatter.11.cloned.1.call-start = ((), (), s32[]{:S(2)}) async-start(), calls=%async_computation.9 | async-start | bytes 327680 | tf_op jit(solution)/shard_map/reduce_scatter | solution.py:97
  131.7 69.2 %copy-start = (f32[128,128]{1,0:T(8,128)S(1)}, f32[128,128]{1,0:T(8,128)}, u32[]{:S(2)}) copy-start(f32[128,128]{1,0:T(8,128)} %get-tuple-element.20) | copy-start | bytes 196612
  136.1 99.8 %reduce-scatter.13.cloned.1.call-start = ((), (), s32[]{:S(2)}) async-start(), calls=%async_computation.10 | async-start | bytes 73728 | tf_op jit(solution)/shard_map/reduce_scatter | solution.py:71
  203.2 87.9 %reduce-scatter.15.cloned.1.call-start = ((), (), s32[]{:S(2)}) async-start(), calls=%async_computation.11 | async-start | bytes 327680 | tf_op jit(solution)/shard_map/reduce_scatter | solution.py:97
  221.6 69.5 %copy-start.1 = (f32[128,128]{1,0:T(8,128)S(1)}, f32[128,128]{1,0:T(8,128)}, u32[]{:S(2)}) copy-start(f32[128,128]{1,0:T(8,128)} %reduce-scatter.11.cloned.1.call-done) | copy-start | bytes 196612
  221.6 69.5 %copy-start.2 = (f32[128,128]{1,0:T(8,128)S(1)}, f32[128,128]{1,0:T(8,128)}, u32[]{:S(2)}) copy-start(f32[128,128]{1,0:T(8,128)} %get-tuple-element.22) | copy-start | bytes 196612
  224.2 101.4 %reduce-scatter.17.cloned.1.call-start = ((), (), s32[]{:S(2)}) async-start(), calls=%async_computation.12 | async-start | bytes 73728 | tf_op jit(solution)/shard_map/reduce_scatter | solution.py:71
  292.9 80.5 %all-gather.2.cloned.1.call-start = ((), (), s32[]{:S(2)}) async-start(), calls=%async_computation.13 | async-start | bytes 2621440 | tf_op jit(solution)/shard_map/all_gather | solution.py:105
  306.9 4.3 %copy-start.8 = (f32[128]{0:T(128)S(1)}, f32[128]{0:T(128)}, u32[]{:S(2)}) copy-start(f32[128]{0:T(128)} %param.10) | copy-start | bytes 1540
  306.9 18.7 %copy-start.3 = (f32[16,128]{1,0:T(8,128)S(1)}, f32[16,128]{1,0:T(8,128)}, u32[]{:S(2)}) copy-start(f32[16,128]{1,0:T(8,128)} %reduce-scatter.13.cloned.1.call-done) | copy-start | bytes 24580
  306.9 18.7 %copy-start.6 = (s32[16]{0:T(128)S(1)}, s32[16]{0:T(128)}, u32[]{:S(2)}) copy-start(s32[16]{0:T(128)} %copy-done.5) | copy-start | bytes 196
Sparse Core Ops, SparseCore 0:
  62.8 23.8 reduce-scatter.6
  113.6 31.7 reduce-scatter.8
  148.2 19.9 reduce-scatter.10
  203.3 32.4 reduce-scatter.12
  238.5 19.9 reduce-scatter.14
  293.0 32.5 reduce-scatter.16
  327.7 45.6 all-gather.1
where the time goes:
time: 385 us; the launch traced here: 384 us
  blocking collectives  195 us (51%)
  waiting for transfers between devices  85.3 us (22%)
  matrix products  33.9 us (9%)
  other arithmetic  32.9 us (9%)
  between operations  23 us (6%)
  local copies, waits for them, and re-layouts  6.75 us (2%)
  starting transfers between devices  6.6 us (2%)
    psum x2, blocking collectives, per_device(): primal, dual = lax.psum((primal, dual), ('doc', 'feat'))  78.7 us
    all_gather x3, blocking collectives, per_device(): all_solved = lax.all_gather(solved, 'doc', axis=0, tiled=True)  42.2 us
    all_gather x1, waiting for transfers between devices, per_device(): weights = lax.all_gather(num_feat * weights, 'doc', axis=0, tiled=True)  37.8 us
    reduce_scatter x3, waiting for transfers between devices, per_device(): sums = lax.psum_scatter(part, 'feat', scatter_dimension=0, tiled=True)  33.2 us
    all_gather x3, blocking collectives, per_device(): correction = lax.all_gather(correction, 'feat', axis=0, tiled=True)  30.8 us
    all_gather x1, blocking collectives, per_device(): doc_full = lax.all_gather(doc_rows, 'doc', axis=0, tiled=True)  25.3 us
    reduce_scatter x1, waiting for transfers between devices, per_device(): gram = lax.psum_scatter(gram, 'doc', scatter_dimension=0, tiled=True)[0]  14.2 us
    dot_general x3, matrix products, per_device(): lax.dot_general(features, all_solved, (((0,), (0,)), ((), ())), precision...  12.5 us
  transfers between devices with their start and end apart: 8, of which 5 were waited for; matrix products, arithmetic and copies ran while one was open for 7% of the time, Pallas kernels for 0%

commit v1 on v0

--- a/solution.py
+++ b/solution.py
@@ -69,7 +69,14 @@
         applied = residue - solved
         part = target - solved
         sums = lax.psum_scatter(part, "feat", scatter_dimension=0, tiled=True)
-        all_solved = lax.all_gather(solved, "doc", axis=0, tiled=True)
+        size = lax.axis_size("doc")
+        hops = [(i, (i + 1) % size) for i in range(size)]
+        parts = [solved]
+        for hop in range(1, size):
+            parts = [lax.ppermute(parts[0], "doc", hops), *parts]
+        whole = jnp.concatenate(parts, axis=0)
+        offset_2 = (lax.axis_index("doc") + 1) * parts[-1].shape[0]
+        all_solved = jnp.roll(whole, offset_2, axis=0)
         lifted = lax.dot_general(features, all_solved, (((0,), (0,)), ((), ())), precision=HI)
         old_weights = weights
         old_margins = margins

time: 385 us -> 431 us (1.12)
  waiting for transfers between devices: 85.3 us -> 169 us
  blocking collectives: 195 us -> 152 us
    ppermute x0 -> x9, waiting for transfers between devices: none -> 51.6 us  [per_device(): parts = [lax.ppermute(parts[0], 'doc', hops), *parts]]
    all_gather x3 -> x0, blocking collectives: 42.2 us -> none  [per_device(): all_solved = lax.all_gather(solved, 'doc', axis=0, tiled=True)]
    reduce_scatter x3, waiting for transfers between devices: 33.2 us -> 65.4 us  [per_device(): sums = lax.psum_scatter(part, 'feat', scatter_dimension=0, tiled=True)]
  transfers between devices with their start and end apart: 8 -> 17, of which waited for: 5 -> 14; matrix products, arithmetic and copies ran while one was open for 7% -> 6% of each run, Pallas kernels for 0% -> 0%
where the time goes in v1:
time: 431 us; the launch traced here: 430 us
  waiting for transfers between devices  169 us (39%)
  blocking collectives  152 us (35%)
  matrix products  35.7 us (8%)
  other arithmetic  33 us (8%)
  between operations  23.2 us (5%)
  starting transfers between devices  10 us (2%)
  local copies, waits for them, and re-layouts  6.76 us (2%)
    psum x2, blocking collectives, per_device(): primal, dual = lax.psum((primal, dual), ('doc', 'feat'))  78.6 us
    reduce_scatter x3, waiting for transfers between devices, per_device(): sums = lax.psum_scatter(part, 'feat', scatter_dimension=0, tiled=True)  65.4 us
    ppermute x9, waiting for transfers between devices, per_device(): parts = [lax.ppermute(parts[0], 'doc', hops), *parts]  51.6 us
    all_gather x1, waiting for transfers between devices, per_device(): weights = lax.all_gather(num_feat * weights, 'doc', axis=0, tiled=True)  37.8 us
    all_gather x3, blocking collectives, per_device(): correction = lax.all_gather(correction, 'feat', axis=0, tiled=True)  29.9 us
    all_gather x1, blocking collectives, per_device(): doc_full = lax.all_gather(doc_rows, 'doc', axis=0, tiled=True)  25.3 us
    dot_general x3, matrix products, per_device(): lax.dot_general(features, all_solved, (((0,), (0,)), ((), ())), precision...  14.4 us
    reduce_scatter x1, waiting for transfers between devices, per_device(): gram = lax.psum_scatter(gram, 'doc', scatter_dimension=0, tiled=True)[0]  14.2 us
  transfers between devices with their start and end apart: 17, of which 14 were waited for; matrix products, arithmetic and copies ran while one was open for 6% of the time, Pallas kernels for 0%

profile of v1, /device:TPU:0, one launch (start us, length us, event | category | flops | bytes accessed | tf_op | source)
XLA Modules:
  0.0 430.0 jit_solution(1048997528707711899)
XLA Ops:
  9.4 6.3 %all-to-all-start = ((bf16[128,4,1024]{0,2,1:T(8,128)(2,1)}), bf16[128,4,1024]{0,2,1:T(8,128)(2,1)S(1)}, u32[]{:S(2)}, u32[]{:S(2)}) async-start(bf16[128,4,1024]{0,2,1:T(8,128)(2,1)} %bitcast), calls=%async_computation | async-start | bytes 2097152 | tf_op jit(solution)/shard_map/all_to_all | solution.py:36
  15.8 9.2 %all_gather.22 = bf16[128,512]{0,1:T(8,128)(2,1)S(1)} all-gather(bf16[128,64]{0,1:T(8,128)(2,1)S(1)} %copy-done.7), channel_id=1, replica_groups=mesh['doc'=4,'feat'=8] {'feat'}, dimensions={1}, use_global_device_ids=true | all-gather | bytes 147456 | tf_op jit(solution)/shard_map/all_gather | solution.py:34
  25.7 25.3 %all_gather.23 = bf16[512,512]{0,1:T(8,128)(2,1)} all-gather(bf16[128,512]{0,1:T(8,128)(2,1)S(1)} %all_gather.22), channel_id=1, replica_groups=mesh['doc'=4,'feat'=8] {'doc'}, dimensions={0}, use_global_device_ids=true | all-gather | bytes 655360 | tf_op jit(solution)/shard_map/all_gather | solution.py:35
  51.6 8.3 %cosine_multiply_fusion = f32[512,1024]{1,0:T(8,128)S(1)} fusion(bf16[512,512]{0,1:T(8,128)(2,1)} %all_gather.23, bf16[512,1024]{1,0:T(8,128)(2,1)S(1)} %bitcast.35, f32[1024]{0:T(1024)S(1)} %dynamic-slice-done, f32[1024]{0:T(1024)S(1)} %dynamic-slice_multiply_fusion), kind=kOutput, calls=%fused_computation | convolution fusion | flops 537919488 | bytes 3678208 | tf_op jit(solution)/shard_map/dot_general | solution.py:39
  59.9 2.8 fusion.177
  63.1 9.4 %all_gather.21 = f32[128,128]{1,0:T(8,128)S(1)} all-gather(f32[16,128]{1,0:T(8,128)S(1)} %broadcast_multiply_fusion), channel_id=1, replica_groups=mesh['doc'=4,'feat'=8] {'feat'}, dimensions={0}, use_global_device_ids=true | all-gather | bytes 73728 | tf_op jit(solution)/shard_map/all_gather | solution.py:65
  72.5 14.2 %reduce-scatter.7.cloned.1.call-done = f32[1,128,128]{2,1,0:T(8,128)} async-done(((f32[4,128,128]{2,1,0:T(8,128)}), f32[1,128,128]{2,1,0:T(8,128)}) %reduce-scatter.7.cloned.1.call-update) | async-done | bytes 65552 | tf_op jit(solution)/shard_map/reduce_scatter | solution.py:43
  88.5 11.7 %cholesky.18 = f32[128,128]{1,0:T(8,128)S(1)} custom-call(f32[128,128]{1,0:T(8,128)S(1)} %fusion.42), custom_call_target="Cholesky" | custom-call | tf_op jit(solution)/shard_map/jit(cholesky)/cholesky | solution.py:45
  101.6 9.8 %custom-call.6 = f32[1,128,128]{1,2,0:T(8,128)S(1)} custom-call(f32[1,128,128]{2,1,0:T(8,128)S(1)} %fusion.39), custom_call_target="InvertDiagBlocksLowerTriangular" | custom-call | tf_op jit(solution)/shard_map/triangular_solve | solution.py:46
  113.4 6.1 %collective-permute-done = f32[128,128]{1,0:T(8,128)S(1)} collective-permute-done((f32[128,128]{1,0:T(8,128)S(1)}, f32[128,128]{1,0:T(8,128)S(1)}, u32[]{:S(2)}, u32[]{:S(2)}) %collective-permute-start) | collective-permute-done | bytes 65568 | tf_op jit(solution)/shard_map/ppermute | solution.py:76
  119.4 6.5 %collective-permute-done.1 = f32[128,128]{1,0:T(8,128)S(1)} collective-permute-done((f32[128,128]{1,0:T(8,128)S(1)}, f32[128,128]{1,0:T(8,128)S(1)}, u32[]{:S(2)}, u32[]{:S(2)}) %collective-permute-start.1) | collective-permute-done | bytes 65568 | tf_op jit(solution)/shard_map/ppermute | solution.py:76
  126.3 5.8 %collective-permute-done.2 = f32[128,128]{1,0:T(8,128)S(1)} collective-permute-done((f32[128,128]{1,0:T(8,128)S(1)}, f32[128,128]{1,0:T(8,128)S(1)}, u32[]{:S(2)}, u32[]{:S(2)}) %collective-permute-start.2) | collective-permute-done | bytes 65568 | tf_op jit(solution)/shard_map/ppermute | solution.py:76
  132.0 4.5 %multiply_reduce_fusion.1 = (f32[]{:T(128)}, f32[]{:T(128)}, f32[1024,128]{1,0:T(8,128)S(1)}) fusion(f32[512,1024]{1,0:T(8,128)S(1)} %cosine_multiply_fusion, s32[]{:T(128)S(6)} %select_n.35, f32[128,128]{1,0:T(8,128)S(1)} %collective-permute-done.2, f32[128,128]{1,0:T(8,128)S(1)} %collective-permute-done.1, f32[128,128]{1,0:T(8,128)S(1)} %collective-permute-done, ...), kind=kOutput, calls=%fused_computation.37 | convolution fusion | flops 807337984 | bytes 2883596 | tf_op jit(solution)/shard_map/dot_general | solution.py:80
  139.1 21.9 %reduce-scatter.9.cloned.1.call-done = f32[16,128]{1,0:T(8,128)} async-done(((f32[128,128]{1,0:T(8,128)}), f32[16,128]{1,0:T(8,128)}) %reduce-scatter.9.cloned.1.call-update) | async-done | bytes 8208 | tf_op jit(solution)/shard_map/reduce_scatter | solution.py:71
  167.0 39.3 %all-reduce.1 = (f32[]{:T(128)}, f32[]{:T(128)}) all-reduce(f32[]{:T(128)S(6)} %add.217, f32[]{:T(128)S(6)} %add.219), channel_id=1, replica_groups=mesh['doc'=4,'feat'=8] {'doc','feat'}, use_global_device_ids=true, to_apply=%region_7.9 | all-reduce | flops 2 | bytes 16 | tf_op jit(solution)/shard_map/psum | solution.py:101
  208.3 10.2 %all_gather.24 = f32[128,128]{1,0:T(8,128)S(1)} all-gather(f32[16,128]{1,0:T(8,128)S(1)} %subtract_multiply_fusion.2), channel_id=1, replica_groups=mesh['doc'=4,'feat'=8] {'feat'}, dimensions={0}, use_global_device_ids=true | all-gather | bytes 73728 | tf_op jit(solution)/shard_map/all_gather | solution.py:65
  222.2 4.7 %collective-permute-done.3 = f32[128,128]{1,0:T(8,128)S(1)} collective-permute-done((f32[128,128]{1,0:T(8,128)S(1)}, f32[128,128]{1,0:T(8,128)S(1)}, u32[]{:S(2)}, u32[]{:S(2)}) %collective-permute-start.3) | collective-permute-done | bytes 65568 | tf_op jit(solution)/shard_map/ppermute | solution.py:76
  226.9 6.1 %collective-permute-done.4 = f32[128,128]{1,0:T(8,128)S(1)} collective-permute-done((f32[128,128]{1,0:T(8,128)S(1)}, f32[128,128]{1,0:T(8,128)S(1)}, u32[]{:S(2)}, u32[]{:S(2)}) %collective-permute-start.4) | collective-permute-done | bytes 65568 | tf_op jit(solution)/shard_map/ppermute | solution.py:76
  233.4 5.8 %collective-permute-done.5 = f32[128,128]{1,0:T(8,128)} collective-permute-done((f32[128,128]{1,0:T(8,128)S(1)}, f32[128,128]{1,0:T(8,128)}, u32[]{:S(2)}, u32[]{:S(2)}) %collective-permute-start.5) | collective-permute-done | bytes 65568 | tf_op jit(solution)/shard_map/ppermute | solution.py:76
  239.2 5.3 %multiply_reduce_fusion = (f32[]{:T(128)}, f32[]{:T(128)}, f32[1024,128]{1,0:T(8,128)S(1)}) fusion(f32[1024,128]{1,0:T(8,128)S(1)} %get-tuple-element.25, f32[]{:T(128)S(6)} %neg.66, f32[]{:T(128)S(6)} %div.199, f32[]{:T(128)S(6)} %pow.6, f32[512,1024]{1,0:T(8,128)S(1)} %cosine_multiply_fusion, s32[]{:T(128)S(6)} %select_n.35, ...), kind=kOutput, calls=%fused_computation.35 | convolution fusion | flops 808648704 | bytes 3407896 | tf_op jit(solution)/shard_map/dot_general | solution.py:80
  244.5 2.5 fusion.172
  247.2 20.0 %reduce-scatter.13.cloned.1.call-done = f32[16,128]{1,0:T(8,128)} async-done(((f32[128,128]{1,0:T(8,128)}), f32[16,128]{1,0:T(8,128)}) %reduce-scatter.13.cloned.1.call-update) | async-done | bytes 8208 | tf_op jit(solution)/shard_map/reduce_scatter | solution.py:71
  271.8 39.3 %all-reduce = (f32[]{:T(128)}, f32[]{:T(128)}) all-reduce(f32[]{:T(128)S(6)} %add.233, f32[]{:T(128)S(6)} %add.235), channel_id=1, replica_groups=mesh['doc'=4,'feat'=8] {'doc','feat'}, use_global_device_ids=true, to_apply=%region_16.18 | all-reduce | flops 2 | bytes 16 | tf_op jit(solution)/shard_map/psum | solution.py:101
  313.2 10.2 %all_gather.25 = f32[128,128]{1,0:T(8,128)S(1)} all-gather(f32[16,128]{1,0:T(8,128)S(1)} %subtract_multiply_fusion.1), channel_id=1, replica_groups=mesh['doc'=4,'feat'=8] {'feat'}, dimensions={0}, use_global_device_ids=true | all-gather | bytes 73728 | tf_op jit(solution)/shard_map/all_gather | solution.py:65
  326.6 4.7 %collective-permute-done.6 = f32[128,128]{1,0:T(8,128)S(1)} collective-permute-done((f32[128,128]{1,0:T(8,128)S(1)}, f32[128,128]{1,0:T(8,128)S(1)}, u32[]{:S(2)}, u32[]{:S(2)}) %collective-permute-start.6) | collective-permute-done | bytes 65568 | tf_op jit(solution)/shard_map/ppermute | solution.py:76
  331.3 6.1 %collective-permute-done.7 = f32[128,128]{1,0:T(8,128)S(1)} collective-permute-done((f32[128,128]{1,0:T(8,128)S(1)}, f32[128,128]{1,0:T(8,128)S(1)}, u32[]{:S(2)}, u32[]{:S(2)}) %collective-permute-start.7) | collective-permute-done | bytes 65568 | tf_op jit(solution)/shard_map/ppermute | solution.py:76
  337.6 5.9 %collective-permute-done.8 = f32[128,128]{1,0:T(8,128)S(1)} collective-permute-done((f32[128,128]{1,0:T(8,128)S(1)}, f32[128,128]{1,0:T(8,128)S(1)}, u32[]{:S(2)}, u32[]{:S(2)}) %collective-permute-start.8) | collective-permute-done | bytes 65568 | tf_op jit(solution)/shard_map/ppermute | solution.py:76
  343.5 4.6 %subtract_multiply_fusion = f32[1024,128]{1,0:T(8,128)} fusion(f32[512,1024]{1,0:T(8,128)S(1)} %cosine_multiply_fusion, s32[]{:T(128)S(6)} %select_n.35, f32[128,128]{1,0:T(8,128)S(1)} %collective-permute-done.8, f32[128,128]{1,0:T(8,128)S(1)} %collective-permute-done.7, f32[128,128]{1,0:T(8,128)S(1)} %collective-permute-done.6, ...), kind=kOutput, calls=%fused_computation.34 | convolution fusion | flops 807600128 | bytes 3932180 | tf_op jit(solution)/shard_map/dot_general | solution.py:80
  348.2 23.5 %reduce-scatter.17.cloned.1.call-done = f32[16,128]{1,0:T(8,128)} async-done(((f32[128,128]{1,0:T(8,128)}), f32[16,128]{1,0:T(8,128)}) %reduce-scatter.17.cloned.1.call-update) | async-done | bytes 8208 | tf_op jit(solution)/shard_map/reduce_scatter | solution.py:71
  372.5 9.2 %all_gather.26 = f32[128,128]{1,0:T(8,128)S(1)} all-gather(f32[16,128]{1,0:T(8,128)S(1)} %fusion.92), channel_id=1, replica_groups=mesh['doc'=4,'feat'=8] {'feat'}, dimensions={0}, use_global_device_ids=true | all-gather | bytes 73728 | tf_op jit(solution)/shard_map/all_gather | solution.py:111
  381.7 37.8 %all-gather.2.cloned.1.call-done = f32[4096,128]{1,0:T(8,128)} async-done(((f32[1024,128]{1,0:T(8,128)}), f32[4096,128]{1,0:T(8,128)}) %all-gather.2.cloned.1.call-update) | async-done | bytes 2097168 | tf_op jit(solution)/shard_map/all_gather | solution.py:112
  420.1 3.0 copy.16
  (82 shorter events, 26.6 us)
Async XLA Ops:
  7.2 8.6 %copy-start.7 = (bf16[128,64]{0,1:T(8,128)(2,1)S(1)}, bf16[128,64]{0,1:T(8,128)(2,1)}, u32[]{:S(2)}) copy-start(bf16[128,64]{0,1:T(8,128)(2,1)} %param.8) | copy-start | bytes 49156
  9.4 41.6 %all-to-all-start = ((bf16[128,4,1024]{0,2,1:T(8,128)(2,1)}), bf16[128,4,1024]{0,2,1:T(8,128)(2,1)S(1)}, u32[]{:S(2)}, u32[]{:S(2)}) async-start(bf16[128,4,1024]{0,2,1:T(8,128)(2,1)} %bitcast), calls=%async_computation | async-start | bytes 2097152 | tf_op jit(solution)/shard_map/all_to_all | solution.py:36
  15.8 70.9 %reduce-scatter.7.cloned.1.call-start = ((), (), s32[]{:S(2)}) async-start(), calls=%async_computation.7 | async-start | bytes 327680 | tf_op jit(solution)/shard_map/reduce_scatter | solution.py:43
  15.8 35.8 %dynamic-slice-start = ((f32[4096]{0:T(1024)}, s32[]{:T(128)}), f32[1024]{0:T(1024)S(1)}, s32[]{:S(2)}) async-start(f32[4096]{0:T(1024)} %param.10, s32[]{:T(128)} %select_n.28), calls=%async_computation.14 | async-start | bytes 8704 | tf_op jit(solution)/shard_map/dynamic_slice | solution.py:37
  59.9 2.9 copy-start.12
  59.9 2.9 copy-start.10
  62.7 98.3 %reduce-scatter.9.cloned.1.call-start = ((), (), s32[]{:S(2)}) async-start(), calls=%async_computation.8 | async-start | bytes 73728 | tf_op jit(solution)/shard_map/reduce_scatter | solution.py:71
  62.9 204.4 %copy-start.8 = (s32[16]{0:T(128)}, s32[16]{0:T(128)S(1)}, u32[]{:S(2)}) copy-start(s32[16]{0:T(128)S(1)} %dynamic-slice) | copy-start | bytes 196
  113.4 6.1 %collective-permute-start = (f32[128,128]{1,0:T(8,128)S(1)}, f32[128,128]{1,0:T(8,128)S(1)}, u32[]{:S(2)}, u32[]{:S(2)}) collective-permute-start(f32[128,128]{1,0:T(8,128)S(1)} %get-tuple-element.24), channel_id=1, source_target_pairs={{0,8},{8,16},{16,24},{24,0},{1,9},{9,17},{17,25},{25,1},{2,10},{10... | collective-permute-start | bytes 196616 | tf_op jit(solution)/shard_map/ppermute | solution.py:76
  119.4 6.6 %collective-permute-start.1 = (f32[128,128]{1,0:T(8,128)S(1)}, f32[128,128]{1,0:T(8,128)S(1)}, u32[]{:S(2)}, u32[]{:S(2)}) collective-permute-start(f32[128,128]{1,0:T(8,128)S(1)} %collective-permute-done), channel_id=1, source_target_pairs={{0,8},{8,16},{16,24},{24,0},{1,9},{9,17},{17,25},{25,1},{2,10},{10... | collective-permute-start | bytes 196616 | tf_op jit(solution)/shard_map/ppermute | solution.py:76
  126.0 6.1 %collective-permute-start.2 = (f32[128,128]{1,0:T(8,128)S(1)}, f32[128,128]{1,0:T(8,128)S(1)}, u32[]{:S(2)}, u32[]{:S(2)}) collective-permute-start(f32[128,128]{1,0:T(8,128)S(1)} %collective-permute-done.1), channel_id=1, source_target_pairs={{0,8},{8,16},{16,24},{24,0},{1,9},{9,17},{17,25},{25,1},{2,10},{10... | collective-permute-start | bytes 196616 | tf_op jit(solution)/shard_map/ppermute | solution.py:76
  126.0 92.5 %reduce-scatter.11.cloned.1.call-start = ((), (), s32[]{:S(2)}) async-start(), calls=%async_computation.9 | async-start | bytes 327680 | tf_op jit(solution)/shard_map/reduce_scatter | solution.py:104
  136.5 81.9 %copy-start = (f32[128,128]{1,0:T(8,128)S(1)}, f32[128,128]{1,0:T(8,128)}, u32[]{:S(2)}) copy-start(f32[128,128]{1,0:T(8,128)} %get-tuple-element.21) | copy-start | bytes 196612
  139.1 128.2 %reduce-scatter.13.cloned.1.call-start = ((), (), s32[]{:S(2)}) async-start(), calls=%async_computation.10 | async-start | bytes 73728 | tf_op jit(solution)/shard_map/reduce_scatter | solution.py:71
  220.8 18.4 %copy-start.6 = (f32[128,128]{1,0:T(8,128)}, f32[128,128]{1,0:T(8,128)S(1)}, u32[]{:S(2)}) copy-start(f32[128,128]{1,0:T(8,128)S(1)} %get-tuple-element.26) | copy-start | bytes 196612
  220.8 6.2 %collective-permute-start.3 = (f32[128,128]{1,0:T(8,128)S(1)}, f32[128,128]{1,0:T(8,128)S(1)}, u32[]{:S(2)}, u32[]{:S(2)}) collective-permute-start(f32[128,128]{1,0:T(8,128)S(1)} %get-tuple-element.26), channel_id=1, source_target_pairs={{0,8},{8,16},{16,24},{24,0},{1,9},{9,17},{17,25},{25,1},{2,10},{10... | collective-permute-start | bytes 196616 | tf_op jit(solution)/shard_map/ppermute | solution.py:76
  226.9 6.1 %collective-permute-start.4 = (f32[128,128]{1,0:T(8,128)S(1)}, f32[128,128]{1,0:T(8,128)S(1)}, u32[]{:S(2)}, u32[]{:S(2)}) collective-permute-start(f32[128,128]{1,0:T(8,128)S(1)} %collective-permute-done.3), channel_id=1, source_target_pairs={{0,8},{8,16},{16,24},{24,0},{1,9},{9,17},{17,25},{25,1},{2,10},{10... | collective-permute-start | bytes 196616 | tf_op jit(solution)/shard_map/ppermute | solution.py:76
  233.0 6.2 %collective-permute-start.5 = (f32[128,128]{1,0:T(8,128)S(1)}, f32[128,128]{1,0:T(8,128)}, u32[]{:S(2)}, u32[]{:S(2)}) collective-permute-start(f32[128,128]{1,0:T(8,128)S(1)} %collective-permute-done.4), channel_id=1, source_target_pairs={{0,8},{8,16},{16,24},{24,0},{1,9},{9,17},{17,25},{25,1},{2,10},{10... | collective-permute-start | bytes 196616 | tf_op jit(solution)/shard_map/ppermute | solution.py:76
  233.1 90.3 %reduce-scatter.15.cloned.1.call-start = ((), (), s32[]{:S(2)}) async-start(), calls=%async_computation.11 | async-start | bytes 327680 | tf_op jit(solution)/shard_map/reduce_scatter | solution.py:104
  244.5 78.9 %copy-start.1 = (f32[128,128]{1,0:T(8,128)S(1)}, f32[128,128]{1,0:T(8,128)}, u32[]{:S(2)}) copy-start(f32[128,128]{1,0:T(8,128)} %reduce-scatter.11.cloned.1.call-done) | copy-start | bytes 196612
  244.5 78.9 %copy-start.2 = (f32[128,128]{1,0:T(8,128)S(1)}, f32[128,128]{1,0:T(8,128)}, u32[]{:S(2)}) copy-start(f32[128,128]{1,0:T(8,128)} %get-tuple-element.23) | copy-start | bytes 196612
  247.1 124.6 %reduce-scatter.17.cloned.1.call-start = ((), (), s32[]{:S(2)}) async-start(), calls=%async_computation.12 | async-start | bytes 73728 | tf_op jit(solution)/shard_map/reduce_scatter | solution.py:71
  268.8 54.7 %copy-start.4 = (f32[16,128]{1,0:T(8,128)}, f32[16,128]{1,0:T(8,128)S(1)}, u32[]{:S(2)}) copy-start(f32[16,128]{1,0:T(8,128)S(1)} %get-tuple-element.13) | copy-start | bytes 24580
  325.1 6.2 %collective-permute-start.6 = (f32[128,128]{1,0:T(8,128)S(1)}, f32[128,128]{1,0:T(8,128)S(1)}, u32[]{:S(2)}, u32[]{:S(2)}) collective-permute-start(f32[128,128]{1,0:T(8,128)S(1)} %get-tuple-element.29), channel_id=1, source_target_pairs={{0,8},{8,16},{16,24},{24,0},{1,9},{9,17},{17,25},{25,1},{2,10},{10... | collective-permute-start | bytes 196616 | tf_op jit(solution)/shard_map/ppermute | solution.py:76
  331.3 6.1 %collective-permute-start.7 = (f32[128,128]{1,0:T(8,128)S(1)}, f32[128,128]{1,0:T(8,128)S(1)}, u32[]{:S(2)}, u32[]{:S(2)}) collective-permute-start(f32[128,128]{1,0:T(8,128)S(1)} %collective-permute-done.6), channel_id=1, source_target_pairs={{0,8},{8,16},{16,24},{24,0},{1,9},{9,17},{17,25},{25,1},{2,10},{10... | collective-permute-start | bytes 196616 | tf_op jit(solution)/shard_map/ppermute | solution.py:76
  337.4 6.1 %collective-permute-start.8 = (f32[128,128]{1,0:T(8,128)S(1)}, f32[128,128]{1,0:T(8,128)S(1)}, u32[]{:S(2)}, u32[]{:S(2)}) collective-permute-start(f32[128,128]{1,0:T(8,128)S(1)} %collective-permute-done.7), channel_id=1, source_target_pairs={{0,8},{8,16},{16,24},{24,0},{1,9},{9,17},{17,25},{25,1},{2,10},{10... | collective-permute-start | bytes 196616 | tf_op jit(solution)/shard_map/ppermute | solution.py:76
  337.5 10.6 %copy-start.11 = (f32[128]{0:T(128)S(1)}, f32[128]{0:T(128)}, u32[]{:S(2)}) copy-start(f32[128]{0:T(128)} %param.12) | copy-start | bytes 1540
  337.5 34.2 %copy-start.3 = (f32[16,128]{1,0:T(8,128)S(1)}, f32[16,128]{1,0:T(8,128)}, u32[]{:S(2)}) copy-start(f32[16,128]{1,0:T(8,128)} %reduce-scatter.13.cloned.1.call-done) | copy-start | bytes 24580
  337.5 34.2 %copy-start.5 = (f32[16,128]{1,0:T(8,128)S(1)}, f32[16,128]{1,0:T(8,128)}, u32[]{:S(2)}) copy-start(f32[16,128]{1,0:T(8,128)} %copy-done.4) | copy-start | bytes 24580
  337.5 34.1 %copy-start.9 = (s32[16]{0:T(128)S(1)}, s32[16]{0:T(128)}, u32[]{:S(2)}) copy-start(s32[16]{0:T(128)} %copy-done.8) | copy-start | bytes 196
  337.5 82.0 %all-gather.2.cloned.1.call-start = ((), (), s32[]{:S(2)}) async-start(), calls=%async_computation.13 | async-start | bytes 2621440 | tf_op jit(solution)/shard_map/all_gather | solution.py:112
Sparse Core Ops, SparseCore 0:
  62.8 23.8 reduce-scatter.6
  126.1 34.8 reduce-scatter.8
  163.9 19.9 reduce-scatter.10
  233.2 34.0 reduce-scatter.12
  269.9 19.9 reduce-scatter.14
  337.6 34.0 reduce-scatter.16
  373.8 45.6 all-gather.1
